TPU v7x, 32 devices: a whole 2x2x4 slice. The times are simulated.
32 devices in a mesh: rep: 2 (over y), seq: 16 (over z, x, core).
Axes of the slice: x: 2, y: 2, z: 4, core: 2. Of those that a mesh axis runs over, the one named last changes fastest.
Arguments:
- latents: bfloat16 [16, 24576], P(None, ('rep', 'seq')), parts along dimension 1, may hold values from -6 to 6
- layout: int32 [32, 768], P('rep'), parts along dimension 0, may hold values from 0 to 12287, as said below
- assign: int32 [16], P('rep'), parts along dimension 0, may hold values from 0 to 7, as said below
- counts: int32 [16], P('rep'), parts along dimension 0, may hold values from 1 to 3
- latent_cache: bfloat16 [2, 128, 1024], P(None, ('rep', 'seq')), parts along dimension 1, may hold values from -6 to 6
- feature_cache: bfloat16 [2, 128, 64, 384], P(None, ('rep', 'seq')), parts along dimension 1, may hold values from -4 to 4
- first_weight: bfloat16 [3, 3, 3, 16, 384], replicated, may hold values from -0.3125 to 0.3125
- first_bias: float32 [384], replicated, may hold values from -3 to 3
- norm_gain: float32 [384], replicated, may hold values from 0.25 to 1.75
- second_weight: bfloat16 [3, 3, 3, 384, 192], replicated, may hold values from -0.0625 to 0.0625
- second_bias: float32 [192], replicated, may hold values from -3 to 3
Outputs:
- decoded_frames: bfloat16 [3, 256, 128, 192], P(None, ('rep', 'seq')), parts along dimension 1
- latent_cache_next: bfloat16 [2, 128, 1024], P(None, ('rep', 'seq')), parts along dimension 1
- feature_cache_next: bfloat16 [2, 128, 64, 384], P(None, ('rep', 'seq')), parts along dimension 1
There are 2 independent parts, one for each index of `rep`. A program takes and returns all parts, laid end to end along the dimension named above; an argument that names none is the same for every part. Nothing has to cross between parts.
Inputs may be any that keep to these rules, and one draw needn't show every extreme that they name: assign is a permutation of 0 to 7. layout is a permutation of 0 to 12287. Call the cells of request assign[g], rows k * 4 to (k + 1) * 4 - 1, all frames and columns, the tile of seq index (g * 2 + k - 1) mod 16; every row of layout holds exactly 48 cells of every tile.
All inputs are finite; a program needn't handle non-finite values.
Results may differ from a plain program's by a relative error of at most 0.0034.
Values may be sent and summed in bfloat16 or wider, within the bound.
A program may use at most 128 MiB of HBM per device.

v0:
```python
import jax
import jax.numpy as jnp
from jax import lax
from jax.sharding import PartitionSpec as P

LAT_CH = 16
REQS = 8
FMAX = 3
ROWS_DEV = 4
W = 64


def padded_2(array, sides, width):
    for axis, dim in sides:
        devices, length = (lax.axis_size(axis), array.shape[dim])
        up = [(i, (i + 1) % devices) for i in range(devices)]
        down = [(j, i) for i, j in up]
        last = lax.slice_in_dim(array, length - width, length, axis=dim)
        first = lax.slice_in_dim(array, 0, width, axis=dim)
        before = lax.ppermute(last, axis, up)
        after = lax.ppermute(first, axis, down)
        array = jnp.concatenate([before, array, after], axis=dim)
    return array


def tile_numbers(layout, assign, per_group, devices):
    height = ROWS_DEV * per_group
    offset = per_group // 2
    tile_cells = FMAX * ROWS_DEV * W
    column = layout % W
    remain = layout // W
    image_row = remain % height
    remain = remain // height
    frame_index = remain % FMAX
    request = remain // FMAX
    group_ranks = jnp.arange(REQS, dtype=jnp.int32)
    group_index = jnp.sum(jnp.where(assign == request[..., None], group_ranks, 0), axis=-1)
    place = group_index * per_group + image_row // ROWS_DEV
    target = (place - offset + devices) % devices
    within = (frame_index * ROWS_DEV + image_row % ROWS_DEV) * W + column
    return target * tile_cells + within


def keep_rows(values, rim_width, position, height):
    row_index = position * ROWS_DEV - rim_width + jnp.arange(values.shape[1], dtype=jnp.int32)
    inside = (row_index >= 0) & (row_index < height)
    return jnp.where(inside[None, :, None, None], values, jnp.zeros((), values.dtype))


def causal_conv(values, weight, offset):
    result = lax.conv_general_dilated(
        values[None],
        weight,
        (1, 1, 1),
        ((0, 0), (0, 0), (1, 1)),
        dimension_numbers=("NDHWC", "DHWIO", "NDHWC"),
        preferred_element_type=jnp.float32,
    )
    return result[0] + offset


def activate(linear, norm_gain):
    inverse = lax.rsqrt(jnp.mean(linear * linear, axis=-1, keepdims=True) + 1e-06)
    return jax.nn.silu(linear * inverse * norm_gain).astype(jnp.bfloat16)


def body(
    latents,
    layout,
    assign,
    counts,
    latent_cache,
    feature_cache,
    first_weight,
    first_bias,
    norm_gain,
    second_weight,
    second_bias,
):
    devices = lax.axis_size("seq")
    myself = lax.axis_index("seq")
    per_group = devices // REQS
    offset = per_group // 2
    height = ROWS_DEV * per_group
    tile_cells = FMAX * ROWS_DEV * W
    per_peer = tile_cells // devices
    numbers = tile_numbers(layout, assign, per_group, devices)
    own_numbers = lax.dynamic_index_in_dim(numbers, myself, 0, keepdims=False)
    sending_order = jnp.argsort(own_numbers)
    outgoing = jnp.take(latents, sending_order, axis=1).reshape(LAT_CH, devices, per_peer)
    incoming = lax.all_to_all(outgoing, "seq", split_axis=1, concat_axis=1, tiled=True)
    arrived = lax.dynamic_slice_in_dim(jnp.sort(numbers, axis=1), myself * per_peer, per_peer, 1)
    placing = jnp.argsort((arrived - myself * tile_cells).reshape(-1))
    arranged = jnp.take(incoming.reshape(LAT_CH, tile_cells), placing, axis=1)
    window = jnp.transpose(arranged.reshape(LAT_CH, FMAX, ROWS_DEV, W), (1, 2, 3, 0))
    place = (myself + offset) % devices
    position = place % per_group
    request = jnp.take(assign, place // per_group)
    live_frames = jnp.take(counts, request)
    first_input = jnp.concatenate([latent_cache.reshape(2, ROWS_DEV, W, LAT_CH), window], axis=0)
    padded = keep_rows(padded_2(first_input, (("seq", 1),), 2), 2, position, height)
    widened = activate(causal_conv(padded, first_weight, first_bias), norm_gain)
    cached = padded_2(feature_cache, (("seq", 1),), 1)
    extended = keep_rows(jnp.concatenate([cached, widened], axis=0), 1, position, height)
    second_input = extended[:, 1:-1]
    doubled = jnp.repeat(jnp.repeat(extended, 2, axis=1)[:, 1:-1], 2, axis=2)
    decoded = causal_conv(doubled, second_weight, second_bias)
    frame_index = jnp.arange(FMAX, dtype=jnp.int32)[:, None, None, None]
    decoded_frames = jnp.where(frame_index < live_frames, decoded, 0.0).astype(jnp.bfloat16)
    latent_next = lax.dynamic_slice_in_dim(first_input, live_frames, 2, 0).reshape(
        2, ROWS_DEV, W * LAT_CH
    )
    feature_next = lax.dynamic_slice_in_dim(second_input, live_frames, 2, 0)
    return (decoded_frames, latent_next, feature_next)


def solution(mesh):
    return jax.shard_map(
        body,
        mesh=mesh,
        in_specs=(
            P(None, ("rep", "seq")),
            P("rep", None),
            P("rep"),
            P("rep"),
            P(None, ("rep", "seq"), None),
            P(None, ("rep", "seq"), None, None),
            P(),
            P(),
            P(),
            P(),
            P(),
        ),
        out_specs=(
            P(None, ("rep", "seq"), None, None),
            P(None, ("rep", "seq"), None),
            P(None, ("rep", "seq"), None, None),
        ),
        check_vma=False,
    )
```

profile of v0, /device:TPU:0, one launch (start us, length us, event | category | flops | bytes accessed | tf_op | source)
XLA Modules:
  0.0 125.3 jit_solution(521150394125300749)
XLA Ops:
  7.2 0.0 copy-start
  7.2 0.0 sort.43.cloned.1.call-start
  7.3 0.9 add_select_fusion.6
  8.2 0.8 select_reduce_fusion
  9.0 1.6 %fusion.29 = s32[16,768]{1,0:T(8,128)} fusion(s32[16,768]{1,0:T(8,128)S(1)} %select_reduce_fusion, s32[16,768]{1,0:T(8,128)} %param.14), kind=kLoop, calls=%fused_computation.67 | loop fusion | flops 1019904 | bytes 147456 | tf_op jit(solution)/shard_map/add | solution.py:41
  10.6 0.0 sort.43.cloned.1.call-update
  10.7 0.8 dynamic-slice_reduce_fusion
  11.4 4.4 %sort.39 = (s32[768]{0:T(1024)}, s32[768]{0:T(1024)S(1)}) sort(s32[768]{0:T(1024)S(1)} %dynamic-slice_reduce_fusion, s32[768]{0:T(1024)S(1)} %iota.27), dimensions={0}, to_apply=%region_1.2 | sort | flops 7680 | bytes 12288 | tf_op jit(solution)/shard_map/jit(argsort)/sort | solution.py:89
  15.8 0.9 copy.92
  16.7 1.9 %gather_fusion = bf16[768,16]{1,0:T(8,128)(2,1)S(1)} fusion(bf16[16,768]{0,1:T(8,128)(2,1)S(1)} %copy.92, s32[1024]{0:T(1024)S(1)} %pad_clamp_fusion.1), kind=kCustom, calls=%fused_computation.clone | custom fusion | bytes 52224 | tf_op jit(solution)/shard_map/jit(_take)/gather | solution.py:90
  18.6 0.2 broadcast_select_fusion.1
  18.8 0.1 copy.93
  18.9 0.7 reshape.223
  19.7 7.4 %all-to-all-start = ((bf16[16,2,384]{2,1,0:T(2,128)(2,1)}), bf16[16,2,384]{2,1,0:T(2,128)(2,1)S(1)}, u32[]{:S(2)}, u32[]{:S(2)}) async-start(bf16[16,2,384]{2,1,0:T(2,128)(2,1)} %reshape.223), calls=%async_computation | async-start | bytes 49152 | tf_op jit(solution)/shard_map/all_to_all | solution.py:91
  27.1 1.3 %copy.89 = bf16[2,4,64,384]{3,1,2,0:T(4,128)(2,1)S(1)} copy(bf16[2,4,64,384]{3,2,1,0:T(8,128)(2,1)} %param.18) | data formatting | bytes 786432 | tf_op args[5]
  28.4 1.0 fusion.49
  29.4 0.4 collective-permute-start
  29.8 4.0 %collective-permute-start.1 = (bf16[2,1,64,384]{3,1,2,0:T(2,128)(2,1)}, bf16[2,1,64,384]{3,1,2,0:T(2,128)(2,1)}, u32[]{:S(2)}, u32[]{:S(2)}) collective-permute-start(bf16[2,1,64,384]{3,1,2,0:T(2,128)(2,1)} %get-tuple-element.46), channel_id=1, source_target_pairs={{1,0},{2,1},{3,2},{4,3},{5,4},{6,5},{7,6},{8,7},{9,8},{10,9},{11,1... | collective-permute-start | bytes 294920 | tf_op jit(solution)/shard_map/ppermute | solution.py:21
  33.8 0.7 dynamic-slice.4
  35.3 0.7 dynamic-slice.5
  36.6 0.1 reshape.108
  36.8 0.1 copy.96
  36.9 0.0 sort.43.cloned.1.call-done
  36.9 0.8 dynamic-slice_subtract_fusion
  37.7 0.1 reshape.111
  37.8 4.4 %sort.41 = (s32[768]{0:T(1024)}, s32[768]{0:T(1024)S(1)}) sort(s32[768]{0:T(1024)S(1)} %reshape.111, s32[768]{0:T(1024)S(1)} %iota.28), dimensions={0}, to_apply=%region_3.5 | sort | flops 7680 | bytes 12288 | tf_op jit(solution)/shard_map/jit(argsort)/sort | solution.py:93
  42.2 0.1 reshape.224
  42.3 0.1 copy.94
  42.5 1.9 %gather_fusion.1 = bf16[768,16]{1,0:T(8,128)(2,1)S(1)} fusion(bf16[16,768]{0,1:T(8,128)(2,1)S(1)} %bitcast.62, s32[1024]{0:T(1024)S(1)} %pad_clamp_fusion), kind=kCustom, calls=%fused_computation.1.clone | custom fusion | bytes 52224 | tf_op jit(solution)/shard_map/jit(_take)/gather | solution.py:94
  44.4 0.2 broadcast_select_fusion
  44.6 0.1 copy.95
  44.7 0.1 collective-permute-start.2
  44.8 4.4 %collective-permute-start.3 = (bf16[5,2,64,16]{2,3,1,0:T(8,128)(2,1)S(1)}, bf16[5,2,64,16]{2,3,1,0:T(8,128)(2,1)S(1)}, u32[]{:S(2)}, u32[]{:S(2)}) collective-permute-start(bf16[5,2,64,16]{2,3,1,0:T(8,128)(2,1)S(1)} %get-tuple-element.48), channel_id=1, source_target_pairs={{1,0},{2,1},{3,2},{4,3},{5,4},{6,5},{7,6},{8,7},{9,8},{10,9},{11,1... | collective-permute-start | bytes 61448 | tf_op jit(solution)/shard_map/ppermute | solution.py:21
  49.3 0.1 copy.107
  49.4 0.8 reshape.114
  50.2 0.7 collective-permute-done.2
  51.0 0.4 copy.97
  51.4 0.1 select_bitcast_fusion
  51.5 0.1 pad.4
  51.6 0.1 copy.99
  51.8 1.8 %convolution_select_fusion = f32[3,6,8,9,384]{4,2,3,1,0:T(8,128)S(1)} fusion(bf16[3,3,3,16,384]{4,3,2,1,0:T(8,128)(2,1)S(1)} %copy-done, pred[8,9]{0,1:T(8,128)(4,1)S(1)} %copy-done.9, bf16[5,8,1,7,2,16]{5,3,4,1,0,2:T(8,128)(2,1)S(1)} %slice.48, bf16[5,8,1,8,9,16]{5,3,4,1,0,2:T(8,128)(2,1)S(1)} %copy.99), kind=kOutput, calls=%fused_computation.23 | convolution fusion | flops 430817280 | bytes 2432584 | tf_op jit(solution)/shard_map/conv_general_dilated | solution.py:51
  53.7 0.5 copy.100
  54.2 0.2 copy-done.2
  54.3 0.4 multiply_reduce_fusion
  54.7 0.1 copy.101
  54.8 0.1 copy.102
  55.0 0.7 multiply_convert_fusion
  55.7 2.0 %maximum_select_fusion = bf16[5,6,64,384]{3,1,2,0:T(8,128)(2,1)S(1)} fusion(bf16[3,6,64,384]{3,1,2,0:T(8,128)(2,1)S(1)} %multiply_convert_fusion, bf16[2,1,64,384]{3,1,2,0:T(2,128)(2,1)} %collective-permute-done.1, bf16[2,4,64,384]{3,1,2,0:T(4,128)(2,1)S(1)} %copy.89, bf16[2,1,64,384]{3,1,2,0:T(2,128)(2,1)} %collective-permute-done, ...), kind=kLoop, calls=%fused_computation.19 | loop fusion | flops 6635520 | bytes 2949126 | tf_op jit(solution)/shard_map/jit(_where)/select_n | solution.py:47
  57.8 0.5 slice.53
  58.3 0.3 copy.103
  58.6 0.1 constant_dynamic-slice_fusion
  58.8 0.8 copy.109
  59.5 0.5 broadcast_in_dim.85
  60.0 0.3 slice.50
  60.3 4.4 %broadcast_in_dim.86 = bf16[5,10,64,2,384]{4,3,2,1,0:T(2,128)(2,1)} broadcast(bf16[5,10,64,384]{3,2,1,0:T(8,128)(2,1)S(1)} %slice.50), dimensions={0,1,2,4} | broadcast | bytes 7372800 | tf_op jit(solution)/shard_map/broadcast_in_dim | solution.py:106
  64.7 11.0 %reshape.191 = bf16[5,10,1,128,384]{4,3,1,0,2:T(8,128)(2,1)} reshape(bf16[5,10,64,2,384]{4,3,2,1,0:T(2,128)(2,1)} %broadcast_in_dim.86) | data formatting | bytes 9830400 | tf_op jit(solution)/shard_map/broadcast_in_dim;reshape | solution.py:52
  75.7 7.3 %pad.6 = bf16[5,10,1,136,384]{4,3,1,0,2:T(8,128)(2,1)} pad(bf16[5,10,1,128,384]{4,3,1,0,2:T(8,128)(2,1)} %reshape.191, bf16[]{:T(256)} %constant.181.clone.1), padding=0_0x0_0x0_0x1_7x0_0 | pad | bytes 10137602 | tf_op jit(solution)/shard_map/broadcast_in_dim;reshape | solution.py:52
  83.0 8.9 %reshape.166 = bf16[5,10,1,8,17,384]{5,4,3,1,0,2:T(8,128)(2,1)} reshape(bf16[5,10,1,136,384]{4,3,1,0,2:T(8,128)(2,1)} %pad.6) | data formatting | bytes 10444800 | tf_op jit(solution)/shard_map/conv_general_dilated | solution.py:51
  91.9 4.1 %copy.105 = bf16[5,10,1,8,17,384]{5,3,4,1,0,2:T(8,128)(2,1)S(1)} copy(bf16[5,10,1,8,17,384]{5,4,3,1,0,2:T(8,128)(2,1)} %reshape.166) | data formatting | bytes 10444800 | tf_op jit(solution)/shard_map/conv_general_dilated | solution.py:51
  96.0 0.2 slice.51
  96.2 18.6 %fusion.13 = f32[3,8,8,17,192]{4,2,3,1,0:T(8,128)S(1)} fusion(bf16[3,3,3,384,192]{3,4,2,1,0:T(8,128)(2,1)S(1)} %copy-done.6, bf16[5,10,1,7,2,384]{5,3,4,1,0,2:T(8,128)(2,1)S(1)} %slice.51, bf16[5,10,1,8,17,384]{5,3,4,1,0,2:T(8,128)(2,1)S(1)} %copy.105, pred[8,17]{0,1:T(8,128)(4,1)S(1)} %copy-done.8), kind=kOutput, calls=%fused_computation.20 | convolution fusion | flops 13013139456 | bytes 12248200 | tf_op jit(solution)/shard_map/conv_general_dilated | solution.py:51
  114.9 1.1 copy.106
  116.0 0.6 fusion.10
  116.6 1.8 %copy.108 = bf16[3,8,128,192]{2,3,1,0:T(8,128)(2,1)} copy(bf16[3,8,128,192]{3,1,2,0:T(8,128)(2,1)S(1)} %fusion.10) | data formatting | bytes 2359296
  (39 shorter events, 0.3 us)
Async XLA Ops:
  7.2 44.6 %copy-start = (bf16[3,3,3,16,384]{4,3,2,1,0:T(8,128)(2,1)S(1)}, bf16[3,3,3,16,384]{4,3,2,1,0:T(8,128)(2,1)}, u32[]{:S(2)}) copy-start(bf16[3,3,3,16,384]{4,3,2,1,0:T(8,128)(2,1)} %param.19) | copy-start | bytes 995332
  7.2 26.7 %copy-start.5 = (s32[8]{0:T(128)S(1)}, s32[8]{0:T(128)}, u32[]{:S(2)}) copy-start(s32[8]{0:T(128)} %param.15) | copy-start | bytes 100
  7.2 28.1 %copy-start.7 = (s32[8]{0:T(128)S(1)}, s32[8]{0:T(128)}, u32[]{:S(2)}) copy-start(s32[8]{0:T(128)} %param.16) | copy-start | bytes 100
  7.2 29.4 %copy-start.1 = (bf16[2,4,1024]{2,1,0:T(4,128)(2,1)S(1)}, bf16[2,4,1024]{2,1,0:T(4,128)(2,1)}, u32[]{:S(2)}) copy-start(bf16[2,4,1024]{2,1,0:T(4,128)(2,1)} %param.17) | copy-start | bytes 49156
  7.2 29.7 %sort.43.cloned.1.call-start = ((), (), s32[]{:S(2)}) async-start(), calls=%async_computation.1 | async-start | bytes 147488 | tf_op jit(solution)/shard_map/jit(sort)/sort | solution.py:92
  19.7 22.6 %all-to-all-start = ((bf16[16,2,384]{2,1,0:T(2,128)(2,1)}), bf16[16,2,384]{2,1,0:T(2,128)(2,1)S(1)}, u32[]{:S(2)}, u32[]{:S(2)}) async-start(bf16[16,2,384]{2,1,0:T(2,128)(2,1)} %reshape.223), calls=%async_computation | async-start | bytes 49152 | tf_op jit(solution)/shard_map/all_to_all | solution.py:91
  29.4 26.3 %collective-permute-start = (bf16[2,1,64,384]{3,1,2,0:T(2,128)(2,1)}, bf16[2,1,64,384]{3,1,2,0:T(2,128)(2,1)}, u32[]{:S(2)}, u32[]{:S(2)}) collective-permute-start(bf16[2,1,64,384]{3,1,2,0:T(2,128)(2,1)} %get-tuple-element.45), channel_id=1, source_target_pairs={{0,1},{1,2},{2,3},{3,4},{4,5},{5,6},{6,7},{7,8},{8,9},{9,10},{10,1... | collective-permute-start | bytes 294920 | tf_op jit(solution)/shard_map/ppermute | solution.py:20
  29.8 25.9 %collective-permute-start.1 = (bf16[2,1,64,384]{3,1,2,0:T(2,128)(2,1)}, bf16[2,1,64,384]{3,1,2,0:T(2,128)(2,1)}, u32[]{:S(2)}, u32[]{:S(2)}) collective-permute-start(bf16[2,1,64,384]{3,1,2,0:T(2,128)(2,1)} %get-tuple-element.46), channel_id=1, source_target_pairs={{1,0},{2,1},{3,2},{4,3},{5,4},{6,5},{7,6},{8,7},{9,8},{10,9},{11,1... | collective-permute-start | bytes 294920 | tf_op jit(solution)/shard_map/ppermute | solution.py:21
  44.7 6.2 %collective-permute-start.2 = (bf16[5,2,64,16]{2,3,1,0:T(8,128)(2,1)S(1)}, bf16[5,2,64,16]{2,3,1,0:T(8,128)(2,1)S(1)}, u32[]{:S(2)}, u32[]{:S(2)}) collective-permute-start(bf16[5,2,64,16]{2,3,1,0:T(8,128)(2,1)S(1)} %get-tuple-element.47), channel_id=1, source_target_pairs={{0,1},{1,2},{2,3},{3,4},{4,5},{5,6},{6,7},{7,8},{8,9},{9,10},{10,1... | collective-permute-start | bytes 61448 | tf_op jit(solution)/shard_map/ppermute | solution.py:20
  44.8 6.1 %collective-permute-start.3 = (bf16[5,2,64,16]{2,3,1,0:T(8,128)(2,1)S(1)}, bf16[5,2,64,16]{2,3,1,0:T(8,128)(2,1)S(1)}, u32[]{:S(2)}, u32[]{:S(2)}) collective-permute-start(bf16[5,2,64,16]{2,3,1,0:T(8,128)(2,1)S(1)} %get-tuple-element.48), channel_id=1, source_target_pairs={{1,0},{2,1},{3,2},{4,3},{5,4},{6,5},{7,6},{8,7},{9,8},{10,9},{11,1... | collective-permute-start | bytes 61448 | tf_op jit(solution)/shard_map/ppermute | solution.py:21
  51.0 0.8 copy-start.9
  53.7 0.7 copy-start.2
  53.7 1.3 %copy-start.3 = (f32[384]{0:T(512)S(1)}, f32[384]{0:T(512)}, u32[]{:S(2)}) copy-start(f32[384]{0:T(512)} %param.21) | copy-start | bytes 4612
  91.9 4.3 %copy-start.6 = (bf16[3,3,3,384,192]{3,4,2,1,0:T(8,128)(2,1)S(1)}, bf16[3,3,3,384,192]{3,4,2,1,0:T(8,128)(2,1)}, u32[]{:S(2)}) copy-start(bf16[3,3,3,384,192]{3,4,2,1,0:T(8,128)(2,1)} %param.22) | copy-start | bytes 11943940
  91.9 4.3 %copy-start.8 = (pred[8,17]{0,1:T(8,128)(4,1)S(1)}, pred[8,17]{0,1:T(8,128)(4,1)}, u32[]{:S(2)}) copy-start(pred[8,17]{0,1:T(8,128)(4,1)} %constant.233) | copy-start | bytes 412
  114.9 1.1 copy-start.4
Sparse Core Ops, SparseCore 0:
  10.8 3.2 sort.45.cloned.1.call-done
  (1 shorter events, 0.0 us)
where the time goes:
time: 126 us; the launch traced here: 125 us
  local copies, waits for them, and re-layouts  54.5 us (43%)
  matrix products  20.5 us (16%)
  other arithmetic  17.4 us (14%)
  starting transfers between devices  16.3 us (13%)
  between operations  15.9 us (13%)
    conv_general_dilated x2, matrix products, causal_conv(): lax.conv_general_dilated(values[None], weight, (1, 1, 1), ((0, 0), (0, 0)...  20.5 us
    another operation x2, local copies, waits for them, and re-layouts, causal_conv(): values[None]  18.3 us
    conv_general_dilated x7, local copies, waits for them, and re-layouts, causal_conv(): lax.conv_general_dilated(values[None], weight, (1, 1, 1), ((0, 0), (0, 0)...  14.9 us
    ppermute x2, starting transfers between devices, padded_2(): after = lax.ppermute(first, axis, down)  8.47 us
    all_to_all x1, starting transfers between devices, body(): lax.all_to_all(outgoing, 'seq', split_axis=1, concat_axis=1, tiled=True)  7.39 us
    unnamed x27, local copies, waits for them, and re-layouts  5.92 us
    broadcast_in_dim x2, local copies, waits for them, and re-layouts, body(): doubled = jnp.repeat(jnp.repeat(extended, 2, axis=1)[:, 1:-1], 2, axis=2)  4.87 us
    sort x1, other arithmetic, body(): placing = jnp.argsort((arrived - myself * tile_cells).reshape(-1))  4.37 us
  transfers between devices with their start and end apart: 5, of which 1 were waited for; matrix products, arithmetic and copies ran while one was open for 14% of the time, Pallas kernels for 0%

commit v1 on v0

--- a/solution.py
+++ b/solution.py
@@ -1,6 +1,8 @@
 import jax
 import jax.numpy as jnp
 from jax import lax
+from jax.experimental import pallas as pl
+from jax.experimental.pallas import tpu as pltpu
 from jax.sharding import PartitionSpec as P
 
 LAT_CH = 16
@@ -62,6 +64,133 @@
 def activate(linear, norm_gain):
     inverse = lax.rsqrt(jnp.mean(linear * linear, axis=-1, keepdims=True) + 1e-06)
     return jax.nn.silu(linear * inverse * norm_gain).astype(jnp.bfloat16)
+
+
+def decode_kernel(info, cached, fresh, weight, bias, out, carry, shifted, packed, even, odd):
+    frame = pl.program_id(0)
+    rows, columns, mid = fresh.shape[1:]
+    width = bias.shape[-1]
+    lanes = packed.shape[-1]
+    history = cached.shape[0]
+
+    @pl.when(frame == 0)
+    def _prepare():
+        def pack(step, _):
+            at = pl.multiple_of(step * 16, 16)
+            for a in range(3):
+                taps = [
+                    [weight[a, b, e, pl.ds(at, 16), :].astype(jnp.float32) for e in range(3)]
+                    for b in range(3)
+                ]
+                for py in range(2):
+                    if py == 0:
+                        lines = (taps[0], [taps[1][e] + taps[2][e] for e in range(3)])
+                    else:
+                        lines = ([taps[0][e] + taps[1][e] for e in range(3)], taps[2])
+                    for px in range(2):
+                        for iy, line in enumerate(lines):
+                            if px == 0:
+                                pair = (line[0], line[1] + line[2])
+                            else:
+                                pair = (line[0] + line[1], line[2])
+                            for ix, value in enumerate(pair):
+                                start = ((a * 2 + iy) * 2 + ix) * mid
+                                packed[2 * py + px, pl.ds(start + at, 16), 0:width] = value.astype(
+                                    jnp.bfloat16
+                                )
+                                packed[2 * py + px, pl.ds(start + at, 16), width:lanes] = jnp.zeros(
+                                    (16, lanes - width), jnp.bfloat16
+                                )
+            return 0
+
+        lax.fori_loop(0, mid // 16, pack, 0)
+        edge = lax.broadcasted_iota(jnp.int32, (columns, mid), 0)
+        for source, count, first in ((cached, history, 0), (fresh, fresh.shape[0], history)):
+            def shift(step, _):
+                f = step // rows
+                r = step % rows
+                bad = ((r == 0) & (info[0] == 0)) | ((r == rows - 1) & (info[1] == 0))
+                value = jnp.where(bad, 0.0, source[f, r].astype(jnp.float32))
+                left = jnp.where(edge == 0, 0.0, pltpu.roll(value, 1, 0))
+                right = jnp.where(edge == columns - 1, 0.0, pltpu.roll(value, columns - 1, 0))
+                shifted[0, first + f, r] = left.astype(jnp.bfloat16)
+                shifted[1, first + f, r] = value.astype(jnp.bfloat16)
+                shifted[2, first + f, r] = right.astype(jnp.bfloat16)
+                return 0
+
+            lax.fori_loop(0, count * rows, shift, 0)
+        for i in range(history):
+            carry[i] = shifted[1, info[2] + i, 1 : rows - 1]
+
+    inner = rows - 2
+    cells = inner * columns
+    live = frame < info[2]
+    for py in range(2):
+        for px in range(2):
+            parts = []
+            for a in range(3):
+                for iy in range(2):
+                    for ix in range(2):
+                        block = shifted[px + ix, frame + a, py + iy : py + iy + inner]
+                        parts.append(block.reshape(cells, mid))
+            total = jnp.dot(
+                jnp.concatenate(parts, axis=1),
+                packed[2 * py + px],
+                preferred_element_type=jnp.float32,
+            )
+            even[pl.ds(px, cells, stride=2), :] = total[:, 0:128]
+            odd[pl.ds(px, cells, stride=2), :] = total[:, 128:256]
+        for i in range(inner):
+            span = pl.ds(i * 2 * columns, 2 * columns)
+            low = even[span, :] + bias[:, 0:128]
+            high = odd[span, 0 : width - 128] + bias[:, 128:width]
+            out[0, 2 * i + py, :, 0:128] = jnp.where(live, low, 0.0).astype(jnp.bfloat16)
+            out[0, 2 * i + py, :, 128:width] = jnp.where(live, high, 0.0).astype(jnp.bfloat16)
+
+
+def decode(info, cached, fresh, weight, bias):
+    history, rows, columns, mid = cached.shape
+    width = bias.shape[-1]
+    inner = rows - 2
+    frames = fresh.shape[0]
+    lanes = 256
+    return pl.pallas_call(
+        decode_kernel,
+        grid=(frames,),
+        in_specs=[
+            pl.BlockSpec(memory_space=pltpu.SMEM),
+            pl.BlockSpec(cached.shape, lambda t: (0, 0, 0, 0)),
+            pl.BlockSpec(fresh.shape, lambda t: (0, 0, 0, 0)),
+            pl.BlockSpec(weight.shape, lambda t: (0, 0, 0, 0, 0)),
+            pl.BlockSpec((1, width), lambda t: (0, 0)),
+        ],
+        out_specs=[
+            pl.BlockSpec((1, 2 * inner, 2 * columns, width), lambda t: (t, 0, 0, 0)),
+            pl.BlockSpec((history, inner, columns, mid), lambda t: (0, 0, 0, 0)),
+        ],
+        out_shape=[
+            jax.ShapeDtypeStruct((frames, 2 * inner, 2 * columns, width), jnp.bfloat16),
+            jax.ShapeDtypeStruct((history, inner, columns, mid), jnp.bfloat16),
+        ],
+        scratch_shapes=[
+            pltpu.VMEM((3, history + frames, rows, columns, mid), jnp.bfloat16),
+            pltpu.VMEM((4, 12 * mid, lanes), jnp.bfloat16),
+            pltpu.VMEM((2 * inner * columns, 128), jnp.float32),
+            pltpu.VMEM((2 * inner * columns, 128), jnp.float32),
+        ],
+        compiler_params=pltpu.CompilerParams(
+            dimension_semantics=("arbitrary",), vmem_limit_bytes=56 * 1024 * 1024
+        ),
+        cost_estimate=pl.CostEstimate(
+            flops=2 * frames * inner * columns * 48 * mid * lanes,
+            bytes_accessed=8_000_000,
+            transcendentals=0,
+        ),
+    )(info, cached, fresh, weight, bias[None])
+
+
+def one_hot(values, count, dtype=jnp.bfloat16):
+    return (values[..., None] == jnp.arange(count, dtype=jnp.int32)).astype(dtype)
 
 
 def body(
@@ -86,12 +215,30 @@
     per_peer = tile_cells // devices
     numbers = tile_numbers(layout, assign, per_group, devices)
     own_numbers = lax.dynamic_index_in_dim(numbers, myself, 0, keepdims=False)
-    sending_order = jnp.argsort(own_numbers)
-    outgoing = jnp.take(latents, sending_order, axis=1).reshape(LAT_CH, devices, per_peer)
+    send_rank = jnp.sum((own_numbers[None, :] < own_numbers[:, None]).astype(jnp.int32), axis=1)
+    outgoing = jnp.dot(latents, one_hot(send_rank, tile_cells)).reshape(LAT_CH, devices, per_peer)
     incoming = lax.all_to_all(outgoing, "seq", split_axis=1, concat_axis=1, tiled=True)
-    arrived = lax.dynamic_slice_in_dim(jnp.sort(numbers, axis=1), myself * per_peer, per_peer, 1)
-    placing = jnp.argsort((arrived - myself * tile_cells).reshape(-1))
-    arranged = jnp.take(incoming.reshape(LAT_CH, tile_cells), placing, axis=1)
+    inside = numbers - myself * tile_cells
+    mine = (inside >= 0) & (inside < tile_cells)
+    line = jnp.where(mine, inside // W, -1)
+    held = jnp.einsum(
+        "sph,spl->shl",
+        one_hot(line, FMAX * ROWS_DEV),
+        one_hot(inside % W, W),
+        preferred_element_type=jnp.float32,
+    ).reshape(devices, tile_cells)
+    cell = jnp.arange(tile_cells, dtype=jnp.int32)
+    before = jnp.dot(
+        held.astype(jnp.bfloat16),
+        (cell[:, None] < cell[None, :]).astype(jnp.bfloat16),
+        preferred_element_type=jnp.float32,
+    )
+    base = jnp.arange(devices, dtype=jnp.float32)[:, None] * per_peer
+    slot = jnp.sum(held * (before + base), axis=0).astype(jnp.int32)
+    arranged = jnp.dot(
+        incoming.reshape(LAT_CH, tile_cells),
+        (cell[:, None] == slot[None, :]).astype(jnp.bfloat16),
+    )
     window = jnp.transpose(arranged.reshape(LAT_CH, FMAX, ROWS_DEV, W), (1, 2, 3, 0))
     place = (myself + offset) % devices
     position = place % per_group
@@ -101,16 +248,17 @@
     padded = keep_rows(padded_2(first_input, (("seq", 1),), 2), 2, position, height)
     widened = activate(causal_conv(padded, first_weight, first_bias), norm_gain)
     cached = padded_2(feature_cache, (("seq", 1),), 1)
-    extended = keep_rows(jnp.concatenate([cached, widened], axis=0), 1, position, height)
-    second_input = extended[:, 1:-1]
-    doubled = jnp.repeat(jnp.repeat(extended, 2, axis=1)[:, 1:-1], 2, axis=2)
-    decoded = causal_conv(doubled, second_weight, second_bias)
-    frame_index = jnp.arange(FMAX, dtype=jnp.int32)[:, None, None, None]
-    decoded_frames = jnp.where(frame_index < live_frames, decoded, 0.0).astype(jnp.bfloat16)
+    info = jnp.stack(
+        [
+            (position > 0).astype(jnp.int32),
+            (position < per_group - 1).astype(jnp.int32),
+            live_frames.astype(jnp.int32),
+        ]
+    )
+    decoded_frames, feature_next = decode(info, cached, widened, second_weight, second_bias)
     latent_next = lax.dynamic_slice_in_dim(first_input, live_frames, 2, 0).reshape(
         2, ROWS_DEV, W * LAT_CH
     )
-    feature_next = lax.dynamic_slice_in_dim(second_input, live_frames, 2, 0)
     return (decoded_frames, latent_next, feature_next)
 
 

time: 126 us -> 69.5 us (0.55)
  local copies, waits for them, and re-layouts: 54.5 us -> 16.5 us
  Pallas kernels: 0 us -> 15.1 us
  between operations: 15.9 us -> 2.21 us
  other arithmetic: 17.4 us -> 7.08 us
  matrix products: 20.5 us -> 10.8 us
    another operation x2 -> x0, local copies, waits for them, and re-layouts: 18.3 us -> none  [causal_conv(): values[None]]
    pallas_call x0 -> x1, Pallas kernels: none -> 15.1 us  [decode(): pl.pallas_call(decode_kernel, grid=(frames,), in_specs=[pl.BlockSpec(memo...]
    conv_general_dilated x7 -> x0, local copies, waits for them, and re-layouts: 14.9 us -> none  [causal_conv(): lax.conv_general_dilated(values[None], weight, (1, 1, 1), ((0, 0), (0, 0)...]
    conv_general_dilated x2 -> x1, matrix products: 20.5 us -> 8.07 us  [causal_conv(): lax.conv_general_dilated(values[None], weight, (1, 1, 1), ((0, 0), (0, 0)...]
    sort x2 -> x0, other arithmetic: 8.74 us -> none  [the longest x1 4.37 us: body(): placing = jnp.argsort((arrived - myself * tile_cells).reshape(-1))]
    unnamed x27 -> x18, local copies, waits for them, and re-layouts: 5.92 us -> 12 us
    broadcast_in_dim x2 -> x0, local copies, waits for them, and re-layouts: 4.87 us -> none  [body(): doubled = jnp.repeat(jnp.repeat(extended, 2, axis=1)[:, 1:-1], 2, axis=2)]
    gather x2 -> x0, local copies, waits for them, and re-layouts: 3.76 us -> none  [the longest x1 1.88 us: body(): arranged = jnp.take(incoming.reshape(LAT_CH, tile_cells), placing, axis=1)]
  transfers between devices with their start and end apart: 5 -> 5, of which waited for: 1 -> 1; matrix products, arithmetic and copies ran while one was open for 14% -> 37% of each run, Pallas kernels for 0% -> 0%
where the time goes in v1:
time: 69.5 us; the launch traced here: 68.9 us
  local copies, waits for them, and re-layouts  16.5 us (24%)
  starting transfers between devices  16.4 us (24%)
  Pallas kernels  15.1 us (22%)
  matrix products  10.8 us (16%)
  other arithmetic  7.08 us (10%)
  between operations  2.21 us (3%)
  waiting for transfers between devices  0.75 us (1%)
    pallas_call x1, Pallas kernels, decode(): pl.pallas_call(decode_kernel, grid=(frames,), in_specs=[pl.BlockSpec(memo...  15.1 us
    unnamed x18, local copies, waits for them, and re-layouts  12 us
    ppermute x2, starting transfers between devices, padded_2(): after = lax.ppermute(first, axis, down)  8.47 us
    conv_general_dilated x1, matrix products, causal_conv(): lax.conv_general_dilated(values[None], weight, (1, 1, 1), ((0, 0), (0, 0)...  8.07 us
    all_to_all x1, starting transfers between devices, body(): lax.all_to_all(outgoing, 'seq', split_axis=1, concat_axis=1, tiled=True)  7.39 us
    convert_element_type x1, other arithmetic, activate(): return jax.nn.silu(linear * inverse * norm_gain).astype(jnp.bfloat16)  1.5 us
  transfers between devices with their start and end apart: 5, of which 1 were waited for; matrix products, arithmetic and copies ran while one was open for 37% of the time, Pallas kernels for 0%

profile of v1, /device:TPU:0, one launch (start us, length us, event | category | flops | bytes accessed | tf_op | source)
XLA Modules:
  0.0 68.9 jit_solution(6161671158312278101)
XLA Ops:
  0.6 0.0 copy-start
  0.6 0.0 copy-start.5
  0.7 0.0 copy-start.6
  0.7 0.9 %add_select_fusion.8 = s32[16,768]{1,0:T(8,128)S(1)} fusion(s32[16,768]{1,0:T(8,128)} %param.12), kind=kLoop, calls=%fused_computation.46 | loop fusion | flops 466944 | bytes 98304 | tf_op jit(solution)/shard_map/jit(floor_divide)/jit(_where)/select_n | solution.py:37
  1.6 0.8 %select_reduce_fusion = s32[16,768]{1,0:T(8,128)S(1)} fusion(s32[16,768]{1,0:T(8,128)S(1)} %add_select_fusion.8, s32[8]{0:T(128)} %param.13), kind=kLoop, calls=%fused_computation.20 | loop fusion | flops 282624 | bytes 98336 | tf_op jit(solution)/shard_map/reduce_sum | solution.py:39
  2.5 1.0 %fusion.20 = (s32[16,768]{1,0:T(8,128)S(1)}, s32[16,768]{1,0:T(8,128)S(1)}) fusion(s32[]{:T(128)S(6)} %mul.63, s32[16,768]{1,0:T(8,128)} %param.12, s32[16,768]{1,0:T(8,128)S(1)} %select_reduce_fusion), kind=kLoop, calls=%fused_computation.64 | loop fusion | flops 1265664 | bytes 196612 | tf_op jit(solution)/shard_map/jit(_where)/select_n | solution.py:223
  3.5 0.4 convert_reduce_fusion
  3.9 1.3 %fusion.8 = bf16[16,768]{1,0:T(8,128)(2,1)S(1)} fusion(bf16[16,768]{1,0:T(8,128)(2,1)} %param.11, s32[768]{0:T(1024)S(1)} %convert_reduce_fusion), kind=kOutput, calls=%fused_computation.16 | convolution fusion | flops 19464192 | bytes 52224 | tf_op jit(solution)/shard_map/dot_general | solution.py:219
  5.2 0.1 reshape.125
  5.3 0.0 copy-start.2
  5.4 0.7 %reshape.192 = bf16[16,2,384]{2,1,0:T(2,128)(2,1)} reshape(bf16[16,16,48]{2,1,0:T(8,128)(2,1)S(1)} %bitcast.34) | data formatting | bytes 49152
  6.1 7.4 %all-to-all-start = ((bf16[16,2,384]{2,1,0:T(2,128)(2,1)}), bf16[16,2,384]{2,1,0:T(2,128)(2,1)S(1)}, u32[]{:S(2)}, u32[]{:S(2)}) async-start(bf16[16,2,384]{2,1,0:T(2,128)(2,1)} %reshape.192), calls=%async_computation | async-start | bytes 49152 | tf_op jit(solution)/shard_map/all_to_all | solution.py:220
  13.5 1.0 %fusion.36 = (bf16[2,1,64,384]{3,2,1,0:T(8,128)(2,1)S(1)}, bf16[2,1,64,384]{3,2,1,0:T(8,128)(2,1)S(1)}) fusion(bf16[2,4,64,384]{3,2,1,0:T(8,128)(2,1)} %param.16), kind=kLoop, calls=%fused_computation.91 | loop fusion | bytes 393216 | tf_op jit(solution)/shard_map/slice | solution.py:20
  14.5 0.5 collective-permute-start
  14.9 4.0 %collective-permute-start.1 = (bf16[2,1,64,384]{3,2,1,0:T(8,128)(2,1)S(1)}, bf16[2,1,64,384]{3,2,1,0:T(8,128)(2,1)S(1)}, u32[]{:S(2)}, u32[]{:S(2)}) collective-permute-start(bf16[2,1,64,384]{3,2,1,0:T(8,128)(2,1)S(1)} %get-tuple-element.44), channel_id=1, source_target_pairs={{1,0},{2,1},{3,2},{4,3},{5,4},{6,5},{7,6},{8,7},{9,8},{10,9},{11,1... | collective-permute-start | bytes 294920 | tf_op jit(solution)/shard_map/ppermute | solution.py:23
  19.0 0.0 copy-done.5
  19.0 0.6 dynamic-slice.4
  20.3 0.0 copy-done.6
  20.3 0.6 dynamic-slice.5
  20.9 0.7 fusion
  21.5 0.1 reshape.124
  21.6 0.2 fusion.7
  21.9 0.4 iota_compare_fusion.4
  22.9 0.6 pad_add_fusion.info
  23.6 0.0 copy-done.2
  23.6 0.1 reshape.123
  23.7 0.1 copy.31
  23.8 8.2 %copy.33.weight = bf16[3,3,3,384,192]{4,3,2,1,0:T(8,128)(2,1)} copy(bf16[3,3,3,384,192]{3,4,2,1,0:T(8,128)(2,1)} %param.20) | data formatting | bytes 7962624 | tf_op args[9]
  32.0 0.0 all-to-all-done
  32.0 0.1 reshape.193
  32.1 0.1 reshape.189
  32.3 0.6 fusion.32
  32.9 0.1 collective-permute-start.2
  33.0 4.4 %collective-permute-start.3 = (bf16[5,2,64,16]{2,3,1,0:T(8,128)(2,1)S(1)}, bf16[5,2,64,16]{2,3,1,0:T(8,128)(2,1)S(1)}, u32[]{:S(2)}, u32[]{:S(2)}) collective-permute-start(bf16[5,2,64,16]{2,3,1,0:T(8,128)(2,1)S(1)} %get-tuple-element.46), channel_id=1, source_target_pairs={{1,0},{2,1},{3,2},{4,3},{5,4},{6,5},{7,6},{8,7},{9,8},{10,9},{11,1... | collective-permute-start | bytes 61448 | tf_op jit(solution)/shard_map/ppermute | solution.py:23
  37.4 0.1 copy.34
  37.5 0.8 %reshape.127 = bf16[2,4,1024]{2,1,0:T(4,128)(2,1)} reshape(bf16[2,4,64,16]{3,2,1,0:T(8,128)(2,1)S(1)} %copy.34) | data formatting | bytes 32768 | tf_op jit(solution)/shard_map/reshape | solution.py:259
  38.3 0.7 %collective-permute-done.2 = bf16[5,2,64,16]{2,3,1,0:T(8,128)(2,1)S(1)} collective-permute-done((bf16[5,2,64,16]{2,3,1,0:T(8,128)(2,1)S(1)}, bf16[5,2,64,16]{2,3,1,0:T(8,128)(2,1)S(1)}, u32[]{:S(2)}, u32[]{:S(2)}) %collective-permute-start.2) | collective-permute-done | bytes 20512 | tf_op jit(solution)/shard_map/ppermute | solution.py:22
  39.1 0.0 collective-permute-done.3
  39.1 0.1 maximum_select_fusion
  39.2 0.9 %copy.32 = bf16[1,5,8,64,16]{4,0,3,2,1:T(2,128)(2,1)S(1)} copy(bf16[1,5,8,64,16]{3,4,2,1,0:T(8,128)(2,1)S(1)} %maximum_select_fusion) | data formatting | bytes 163840 | tf_op jit(solution)/shard_map/jit(_where)/select_n | solution.py:49
  40.0 0.0 copy-done
  40.0 0.0 copy-start.3
  40.0 8.1 %fusion.37 = f32[1,3,6,64,384]{4,0,3,2,1:T(1,128)S(1)} fusion(bf16[1,5,8,64,16]{4,0,3,2,1:T(2,128)(2,1)S(1)} %copy.32, bf16[3,3,3,16,384]{4,3,2,1,0:T(8,128)(2,1)S(1)} %copy-done), kind=kOutput, calls=%fused_computation.93 | convolution fusion | flops 378224640 | bytes 2183168 | tf_op jit(solution)/shard_map/conv_general_dilated | solution.py:53
  48.1 0.0 copy-done.3
  48.1 0.0 copy-start.4
  48.1 0.2 multiply_reduce_fusion
  48.4 0.0 copy-start.1
  48.4 0.4 copy-done.4
  48.8 1.5 %multiply_convert_fusion.fresh = bf16[3,6,64,384]{3,2,1,0:T(8,128)(2,1)} fusion(f32[1,3,6,64,384]{4,0,3,2,1:T(1,128)S(1)} %fusion.37, f32[384]{0:T(512)S(1)} %copy-done.4, f32[3,6,64]{2,1,0:T(8,128)S(1)} %add_rsqrt_fusion, f32[384]{0:T(512)S(1)} %copy-done.3), kind=kLoop, calls=%fused_computation.9 | loop fusion | flops 3538944 | bytes 2661888 | tf_op jit(solution)/shard_map/convert_element_type | solution.py:66
  50.3 0.0 collective-permute-done
  50.3 0.0 collective-permute-done.1
  50.3 0.0 copy-done.1
  50.3 0.9 %pad_maximum_fusion.cached = bf16[2,6,64,384]{3,2,1,0:T(8,128)(2,1)} fusion(bf16[2,1,64,384]{3,2,1,0:T(8,128)(2,1)S(1)} %collective-permute-done.1, bf16[2,4,64,384]{3,2,1,0:T(8,128)(2,1)S(1)} %copy-done.1, bf16[2,1,64,384]{3,2,1,0:T(8,128)(2,1)S(1)} %collective-permute-done), kind=kLoop, calls=%fused_computation.18 | loop fusion | flops 589824 | bytes 1179648 | tf_op jit(solution)/shard_map/concatenate | solution.py:24
  51.2 15.1 %shard_map.130 = (bf16[3,8,128,192]{3,2,1,0:T(8,128)(2,1)}, bf16[2,4,64,384]{3,2,1,0:T(8,128)(2,1)}) custom-call(s32[3]{0:T(128)} %pad_add_fusion.info, bf16[2,6,64,384]{3,2,1,0:T(8,128)(2,1)} %pad_maximum_fusion.cached, bf16[3,6,64,384]{3,2,1,0:T(8,128)(2,1)} %multiply_convert_fusion.fresh, bf16[3,3,3,384,192]{4,3,2,1,0:T(8,128)(2,1)} %copy.33.weight, ...), custom_call_target="tpu_custom_call" | custom-call | flops 7247757312 | bytes 8000000 | tf_op jit(solution)/shard_map/pallas_call | solution.py:157
  66.4 2.5 %copy.35 = bf16[3,8,128,192]{2,3,1,0:T(8,128)(2,1)} copy(bf16[3,8,128,192]{3,2,1,0:T(8,128)(2,1)} %get-tuple-element.38) | data formatting | bytes 2359296
  (11 shorter events, 0.2 us)
Async XLA Ops:
  0.6 39.4 %copy-start = (bf16[3,3,3,16,384]{4,3,2,1,0:T(8,128)(2,1)S(1)}, bf16[3,3,3,16,384]{4,3,2,1,0:T(8,128)(2,1)}, u32[]{:S(2)}) copy-start(bf16[3,3,3,16,384]{4,3,2,1,0:T(8,128)(2,1)} %param.17) | copy-start | bytes 995332
  0.6 18.3 %copy-start.5 = (s32[8]{0:T(128)S(1)}, s32[8]{0:T(128)}, u32[]{:S(2)}) copy-start(s32[8]{0:T(128)} %param.13) | copy-start | bytes 100
  0.7 19.6 %copy-start.6 = (s32[8]{0:T(128)S(1)}, s32[8]{0:T(128)}, u32[]{:S(2)}) copy-start(s32[8]{0:T(128)} %param.14) | copy-start | bytes 100
  5.3 18.2 %copy-start.2 = (bf16[2,4,1024]{2,1,0:T(4,128)(2,1)S(1)}, bf16[2,4,1024]{2,1,0:T(4,128)(2,1)}, u32[]{:S(2)}) copy-start(bf16[2,4,1024]{2,1,0:T(4,128)(2,1)} %param.15) | copy-start | bytes 49156
  6.1 25.9 %all-to-all-start = ((bf16[16,2,384]{2,1,0:T(2,128)(2,1)}), bf16[16,2,384]{2,1,0:T(2,128)(2,1)S(1)}, u32[]{:S(2)}, u32[]{:S(2)}) async-start(bf16[16,2,384]{2,1,0:T(2,128)(2,1)} %reshape.192), calls=%async_computation | async-start | bytes 49152 | tf_op jit(solution)/shard_map/all_to_all | solution.py:220
  14.5 35.8 %collective-permute-start = (bf16[2,1,64,384]{3,2,1,0:T(8,128)(2,1)S(1)}, bf16[2,1,64,384]{3,2,1,0:T(8,128)(2,1)S(1)}, u32[]{:S(2)}, u32[]{:S(2)}) collective-permute-start(bf16[2,1,64,384]{3,2,1,0:T(8,128)(2,1)S(1)} %get-tuple-element.43), channel_id=1, source_target_pairs={{0,1},{1,2},{2,3},{3,4},{4,5},{5,6},{6,7},{7,8},{8,9},{9,10},{10,1... | collective-permute-start | bytes 294920 | tf_op jit(solution)/shard_map/ppermute | solution.py:22
  14.9 35.4 %collective-permute-start.1 = (bf16[2,1,64,384]{3,2,1,0:T(8,128)(2,1)S(1)}, bf16[2,1,64,384]{3,2,1,0:T(8,128)(2,1)S(1)}, u32[]{:S(2)}, u32[]{:S(2)}) collective-permute-start(bf16[2,1,64,384]{3,2,1,0:T(8,128)(2,1)S(1)} %get-tuple-element.44), channel_id=1, source_target_pairs={{1,0},{2,1},{3,2},{4,3},{5,4},{6,5},{7,6},{8,7},{9,8},{10,9},{11,1... | collective-permute-start | bytes 294920 | tf_op jit(solution)/shard_map/ppermute | solution.py:23
  32.9 6.2 %collective-permute-start.2 = (bf16[5,2,64,16]{2,3,1,0:T(8,128)(2,1)S(1)}, bf16[5,2,64,16]{2,3,1,0:T(8,128)(2,1)S(1)}, u32[]{:S(2)}, u32[]{:S(2)}) collective-permute-start(bf16[5,2,64,16]{2,3,1,0:T(8,128)(2,1)S(1)} %get-tuple-element.45), channel_id=1, source_target_pairs={{0,1},{1,2},{2,3},{3,4},{4,5},{5,6},{6,7},{7,8},{8,9},{9,10},{10,1... | collective-permute-start | bytes 61448 | tf_op jit(solution)/shard_map/ppermute | solution.py:22
  33.0 6.1 %collective-permute-start.3 = (bf16[5,2,64,16]{2,3,1,0:T(8,128)(2,1)S(1)}, bf16[5,2,64,16]{2,3,1,0:T(8,128)(2,1)S(1)}, u32[]{:S(2)}, u32[]{:S(2)}) collective-permute-start(bf16[5,2,64,16]{2,3,1,0:T(8,128)(2,1)S(1)} %get-tuple-element.46), channel_id=1, source_target_pairs={{1,0},{2,1},{3,2},{4,3},{5,4},{6,5},{7,6},{8,7},{9,8},{10,9},{11,1... | collective-permute-start | bytes 61448 | tf_op jit(solution)/shard_map/ppermute | solution.py:23
  40.0 8.1 %copy-start.3 = (f32[384]{0:T(512)S(1)}, f32[384]{0:T(512)}, u32[]{:S(2)}) copy-start(f32[384]{0:T(512)} %param.18) | copy-start | bytes 4612
  48.1 0.7 copy-start.4
  48.4 1.9 %copy-start.1 = (bf16[2,4,64,384]{3,2,1,0:T(8,128)(2,1)S(1)}, bf16[2,4,64,384]{3,2,1,0:T(8,128)(2,1)}, u32[]{:S(2)}) copy-start(bf16[2,4,64,384]{3,2,1,0:T(8,128)(2,1)} %param.16) | copy-start | bytes 1179652

commit v2 on v1

--- a/solution.py
+++ b/solution.py
@@ -66,11 +66,10 @@
     return jax.nn.silu(linear * inverse * norm_gain).astype(jnp.bfloat16)
 
 
-def decode_kernel(info, cached, fresh, weight, bias, out, carry, shifted, packed, even, odd):
+def decode_kernel(info, cached, fresh, weight, bias, out, carry, shifted, packed):
     frame = pl.program_id(0)
     rows, columns, mid = fresh.shape[1:]
-    width = bias.shape[-1]
-    lanes = packed.shape[-1]
+    width = bias.shape[0]
     history = cached.shape[0]
 
     @pl.when(frame == 0)
@@ -95,15 +94,12 @@
                                 pair = (line[0] + line[1], line[2])
                             for ix, value in enumerate(pair):
                                 start = ((a * 2 + iy) * 2 + ix) * mid
-                                packed[2 * py + px, pl.ds(start + at, 16), 0:width] = value.astype(
+                                packed[2 * py + px, pl.ds(at, 16), start : start + mid] = value.astype(
                                     jnp.bfloat16
                                 )
-                                packed[2 * py + px, pl.ds(start + at, 16), width:lanes] = jnp.zeros(
-                                    (16, lanes - width), jnp.bfloat16
-                                )
             return 0
 
-        lax.fori_loop(0, mid // 16, pack, 0)
+        lax.fori_loop(0, width // 16, pack, 0)
         edge = lax.broadcasted_iota(jnp.int32, (columns, mid), 0)
         for source, count, first in ((cached, history, 0), (fresh, fresh.shape[0], history)):
             def shift(step, _):
@@ -125,7 +121,12 @@
     inner = rows - 2
     cells = inner * columns
     live = frame < info[2]
+    pair = 2 * columns
+    spot = lax.broadcasted_iota(jnp.int32, (2 * pair, 2 * pair), 0)
+    goal = spot // pair + 2 * (spot % pair)
+    mix = (lax.broadcasted_iota(jnp.int32, (2 * pair, 2 * pair), 1) == goal).astype(jnp.bfloat16)
     for py in range(2):
+        halves = []
         for px in range(2):
             parts = []
             for a in range(3):
@@ -133,27 +134,27 @@
                     for ix in range(2):
                         block = shifted[px + ix, frame + a, py + iy : py + iy + inner]
                         parts.append(block.reshape(cells, mid))
-            total = jnp.dot(
+            total = lax.dot_general(
+                packed[2 * py + px],
                 jnp.concatenate(parts, axis=1),
-                packed[2 * py + px],
+                (((1,), (1,)), ((), ())),
                 preferred_element_type=jnp.float32,
             )
-            even[pl.ds(px, cells, stride=2), :] = total[:, 0:128]
-            odd[pl.ds(px, cells, stride=2), :] = total[:, 128:256]
-        for i in range(inner):
-            span = pl.ds(i * 2 * columns, 2 * columns)
-            low = even[span, :] + bias[:, 0:128]
-            high = odd[span, 0 : width - 128] + bias[:, 128:width]
-            out[0, 2 * i + py, :, 0:128] = jnp.where(live, low, 0.0).astype(jnp.bfloat16)
-            out[0, 2 * i + py, :, 128:width] = jnp.where(live, high, 0.0).astype(jnp.bfloat16)
+            halves.append(jnp.where(live, total + bias[...], 0.0).astype(jnp.bfloat16))
+        for i in range(0, inner, 2):
+            both = jnp.concatenate(
+                [half[:, i * columns : i * columns + pair] for half in halves], axis=1
+            )
+            mixed = jnp.dot(both, mix, preferred_element_type=jnp.float32).astype(jnp.bfloat16)
+            out[0, 2 * i + py] = mixed[:, 0:pair]
+            out[0, 2 * i + 2 + py] = mixed[:, pair : 2 * pair]
 
 
 def decode(info, cached, fresh, weight, bias):
     history, rows, columns, mid = cached.shape
-    width = bias.shape[-1]
+    width = bias.shape[0]
     inner = rows - 2
     frames = fresh.shape[0]
-    lanes = 256
     return pl.pallas_call(
         decode_kernel,
         grid=(frames,),
@@ -162,31 +163,29 @@
             pl.BlockSpec(cached.shape, lambda t: (0, 0, 0, 0)),
             pl.BlockSpec(fresh.shape, lambda t: (0, 0, 0, 0)),
             pl.BlockSpec(weight.shape, lambda t: (0, 0, 0, 0, 0)),
-            pl.BlockSpec((1, width), lambda t: (0, 0)),
+            pl.BlockSpec((width, 1), lambda t: (0, 0)),
         ],
         out_specs=[
-            pl.BlockSpec((1, 2 * inner, 2 * columns, width), lambda t: (t, 0, 0, 0)),
+            pl.BlockSpec((1, 2 * inner, width, 2 * columns), lambda t: (t, 0, 0, 0)),
             pl.BlockSpec((history, inner, columns, mid), lambda t: (0, 0, 0, 0)),
         ],
         out_shape=[
-            jax.ShapeDtypeStruct((frames, 2 * inner, 2 * columns, width), jnp.bfloat16),
+            jax.ShapeDtypeStruct((frames, 2 * inner, width, 2 * columns), jnp.bfloat16),
             jax.ShapeDtypeStruct((history, inner, columns, mid), jnp.bfloat16),
         ],
         scratch_shapes=[
             pltpu.VMEM((3, history + frames, rows, columns, mid), jnp.bfloat16),
-            pltpu.VMEM((4, 12 * mid, lanes), jnp.bfloat16),
-            pltpu.VMEM((2 * inner * columns, 128), jnp.float32),
-            pltpu.VMEM((2 * inner * columns, 128), jnp.float32),
+            pltpu.VMEM((4, width, 12 * mid), jnp.bfloat16),
         ],
         compiler_params=pltpu.CompilerParams(
             dimension_semantics=("arbitrary",), vmem_limit_bytes=56 * 1024 * 1024
         ),
         cost_estimate=pl.CostEstimate(
-            flops=2 * frames * inner * columns * 48 * mid * lanes,
+            flops=2 * frames * inner * columns * 48 * mid * width,
             bytes_accessed=8_000_000,
             transcendentals=0,
         ),
-    )(info, cached, fresh, weight, bias[None])
+    )(info, cached, fresh, weight, bias[:, None])
 
 
 def one_hot(values, count, dtype=jnp.bfloat16):
@@ -255,7 +254,10 @@
             live_frames.astype(jnp.int32),
         ]
     )
-    decoded_frames, feature_next = decode(info, cached, widened, second_weight, second_bias)
+    decoded_frames, feature_next = decode(
+        info, cached, widened, jnp.swapaxes(second_weight, 3, 4), second_bias
+    )
+    decoded_frames = jnp.swapaxes(decoded_frames, 2, 3)
     latent_next = lax.dynamic_slice_in_dim(first_input, live_frames, 2, 0).reshape(
         2, ROWS_DEV, W * LAT_CH
     )

time: 69.5 us -> 60.9 us (0.88)
  local copies, waits for them, and re-layouts: 16.5 us -> 6.63 us
  waiting for transfers between devices: 0.75 us -> 5.08 us
  starting transfers between devices: 16.4 us -> 12.4 us
  Pallas kernels: 15.1 us -> 16.3 us
    unnamed x18, local copies, waits for them, and re-layouts: 12 us -> 1.3 us
    ppermute x2, starting transfers between devices: 8.47 us -> 4.5 us  [padded_2(): after = lax.ppermute(first, axis, down)]
    ppermute x2, waiting for transfers between devices: 0.74 us -> 4.45 us  [padded_2(): before = lax.ppermute(last, axis, up)]
    pallas_call x1, Pallas kernels: 15.1 us -> 16.3 us  [decode(): pl.pallas_call(decode_kernel, grid=(frames,), in_specs=[pl.BlockSpec(memo...]
    broadcast_in_dim x0 -> x1, local copies, waits for them, and re-layouts: none -> 0.77 us  [decode(): bias[:, None]]
  transfers between devices with their start and end apart: 5 -> 5, of which waited for: 1 -> 2; matrix products, arithmetic and copies ran while one was open for 37% -> 29% of each run, Pallas kernels for 0% -> 0%
where the time goes in v2:
time: 60.9 us; the launch traced here: 60.5 us
  Pallas kernels  16.3 us (27%)
  starting transfers between devices  12.4 us (20%)
  matrix products  10.8 us (18%)
  other arithmetic  7.04 us (12%)
  local copies, waits for them, and re-layouts  6.63 us (11%)
  waiting for transfers between devices  5.08 us (8%)
  between operations  2.26 us (4%)
    pallas_call x1, Pallas kernels, decode(): pl.pallas_call(decode_kernel, grid=(frames,), in_specs=[pl.BlockSpec(memo...  16.3 us
    conv_general_dilated x1, matrix products, causal_conv(): lax.conv_general_dilated(values[None], weight, (1, 1, 1), ((0, 0), (0, 0)...  8.07 us
    all_to_all x1, starting transfers between devices, body(): lax.all_to_all(outgoing, 'seq', split_axis=1, concat_axis=1, tiled=True)  7.39 us
    ppermute x2, starting transfers between devices, padded_2(): after = lax.ppermute(first, axis, down)  4.5 us
    ppermute x2, waiting for transfers between devices, padded_2(): before = lax.ppermute(last, axis, up)  4.45 us
    convert_element_type x1, other arithmetic, activate(): return jax.nn.silu(linear * inverse * norm_gain).astype(jnp.bfloat16)  1.5 us
    unnamed x18, local copies, waits for them, and re-layouts  1.3 us
    dot_general x1, matrix products, body(): jnp.dot(latents, one_hot(send_rank, tile_cells))  1.27 us
  transfers between devices with their start and end apart: 5, of which 2 were waited for; matrix products, arithmetic and copies ran while one was open for 29% of the time, Pallas kernels for 0%

profile of v2, /device:TPU:0, one launch (start us, length us, event | category | flops | bytes accessed | tf_op | source)
XLA Modules:
  0.0 60.5 jit_solution(2104391879660307371)
XLA Ops:
  0.6 0.0 copy-start
  0.6 0.0 copy-start.6
  0.7 0.9 %add_select_fusion.8 = s32[16,768]{1,0:T(8,128)S(1)} fusion(s32[16,768]{1,0:T(8,128)} %param.12), kind=kLoop, calls=%fused_computation.46 | loop fusion | flops 466944 | bytes 98304 | tf_op jit(solution)/shard_map/jit(floor_divide)/jit(_where)/select_n | solution.py:37
  1.6 0.8 %select_reduce_fusion = s32[16,768]{1,0:T(8,128)S(1)} fusion(s32[16,768]{1,0:T(8,128)S(1)} %add_select_fusion.8, s32[8]{0:T(128)} %param.13), kind=kLoop, calls=%fused_computation.20 | loop fusion | flops 282624 | bytes 98336 | tf_op jit(solution)/shard_map/reduce_sum | solution.py:39
  2.5 1.0 %fusion.20 = (s32[16,768]{1,0:T(8,128)S(1)}, s32[16,768]{1,0:T(8,128)S(1)}) fusion(s32[]{:T(128)S(6)} %mul.63, s32[16,768]{1,0:T(8,128)} %param.12, s32[16,768]{1,0:T(8,128)S(1)} %select_reduce_fusion), kind=kLoop, calls=%fused_computation.64 | loop fusion | flops 1265664 | bytes 196612 | tf_op jit(solution)/shard_map/jit(_where)/select_n | solution.py:222
  3.5 0.4 convert_reduce_fusion
  3.9 1.3 %fusion.8 = bf16[16,768]{1,0:T(8,128)(2,1)S(1)} fusion(bf16[16,768]{1,0:T(8,128)(2,1)} %param.11, s32[768]{0:T(1024)S(1)} %convert_reduce_fusion), kind=kOutput, calls=%fused_computation.16 | convolution fusion | flops 19464192 | bytes 52224 | tf_op jit(solution)/shard_map/dot_general | solution.py:218
  5.2 0.1 reshape.125
  5.3 0.0 copy-start.7
  5.3 0.0 copy-start.2
  5.4 0.7 %reshape.192 = bf16[16,2,384]{2,1,0:T(2,128)(2,1)} reshape(bf16[16,16,48]{2,1,0:T(8,128)(2,1)S(1)} %bitcast.36) | data formatting | bytes 49152
  6.1 7.4 %all-to-all-start = ((bf16[16,2,384]{2,1,0:T(2,128)(2,1)}), bf16[16,2,384]{2,1,0:T(2,128)(2,1)S(1)}, u32[]{:S(2)}, u32[]{:S(2)}) async-start(bf16[16,2,384]{2,1,0:T(2,128)(2,1)} %reshape.192), calls=%async_computation | async-start | bytes 49152 | tf_op jit(solution)/shard_map/all_to_all | solution.py:219
  13.5 0.0 copy-start.5
  13.5 1.0 %fusion.36 = (bf16[2,1,64,384]{3,2,1,0:T(8,128)(2,1)S(1)}, bf16[2,1,64,384]{3,2,1,0:T(8,128)(2,1)S(1)}) fusion(bf16[2,4,64,384]{3,2,1,0:T(8,128)(2,1)} %param.16), kind=kLoop, calls=%fused_computation.91 | loop fusion | bytes 393216 | tf_op jit(solution)/shard_map/slice | solution.py:20
  14.5 0.5 collective-permute-start
  14.9 4.0 %collective-permute-start.1 = (bf16[2,1,64,384]{3,2,1,0:T(8,128)(2,1)S(1)}, bf16[2,1,64,384]{3,2,1,0:T(8,128)(2,1)S(1)}, u32[]{:S(2)}, u32[]{:S(2)}) collective-permute-start(bf16[2,1,64,384]{3,2,1,0:T(8,128)(2,1)S(1)} %get-tuple-element.32), channel_id=1, source_target_pairs={{1,0},{2,1},{3,2},{4,3},{5,4},{6,5},{7,6},{8,7},{9,8},{10,9},{11,1... | collective-permute-start | bytes 294920 | tf_op jit(solution)/shard_map/ppermute | solution.py:23
  19.1 0.0 copy-done.6
  19.1 0.6 dynamic-slice.4
  20.3 0.7 %fusion = f32[16,12,64]{2,1,0:T(8,128)S(1)} fusion(s32[16,768]{1,0:T(8,128)S(1)} %add_select_fusion, s32[16,768]{1,0:T(8,128)S(1)} %get-tuple-element.29), kind=kOutput, calls=%fused_computation.1 | convolution fusion | flops 19808256 | bytes 147456 | tf_op jit(solution)/shard_map/sph,spl->shl/dot_general | solution.py:223
  21.0 0.1 reshape.124
  21.1 0.2 fusion.7
  21.4 0.4 iota_compare_fusion.4
  21.8 0.0 copy-done.7
  21.8 0.6 dynamic-slice.5
  23.0 0.6 pad_add_fusion.info
  23.6 0.0 copy-done.2
  23.6 0.1 reshape.123
  23.7 0.1 copy.27
  23.8 0.0 copy-done.5
  23.8 0.8 %copy.29.bias = f32[192,1]{1,0:T(8,128)} copy(f32[192,1]{0,1:T(1,128)S(1)} %bitcast.40) | data formatting | bytes 1536 | tf_op jit(solution)/shard_map/broadcast_in_dim | solution.py:188
  24.6 0.0 all-to-all-done
  24.6 0.1 reshape.193
  24.8 0.1 reshape.189
  24.9 0.6 fusion.32
  25.5 0.5 collective-permute-start.3
  26.0 0.1 collective-permute-start.2
  26.1 0.1 copy.30
  26.2 0.8 %reshape.127 = bf16[2,4,1024]{2,1,0:T(4,128)(2,1)} reshape(bf16[2,4,64,16]{3,2,1,0:T(8,128)(2,1)S(1)} %copy.30) | data formatting | bytes 32768 | tf_op jit(solution)/shard_map/reshape | solution.py:261
  27.0 0.6 %collective-permute-done.3 = bf16[5,2,64,16]{2,3,1,0:T(8,128)(2,1)S(1)} collective-permute-done((bf16[5,2,64,16]{2,3,1,0:T(8,128)(2,1)S(1)}, bf16[5,2,64,16]{2,3,1,0:T(8,128)(2,1)S(1)}, u32[]{:S(2)}, u32[]{:S(2)}) %collective-permute-start.3) | collective-permute-done | bytes 20512 | tf_op jit(solution)/shard_map/ppermute | solution.py:23
  27.7 4.4 %collective-permute-done.2 = bf16[5,2,64,16]{2,3,1,0:T(8,128)(2,1)S(1)} collective-permute-done((bf16[5,2,64,16]{2,3,1,0:T(8,128)(2,1)S(1)}, bf16[5,2,64,16]{2,3,1,0:T(8,128)(2,1)S(1)}, u32[]{:S(2)}, u32[]{:S(2)}) %collective-permute-start.2) | collective-permute-done | bytes 20512 | tf_op jit(solution)/shard_map/ppermute | solution.py:22
  32.1 0.1 maximum_select_fusion
  32.2 0.9 %copy.28 = bf16[1,5,8,64,16]{4,0,3,2,1:T(2,128)(2,1)S(1)} copy(bf16[1,5,8,64,16]{3,4,2,1,0:T(8,128)(2,1)S(1)} %maximum_select_fusion) | data formatting | bytes 163840 | tf_op jit(solution)/shard_map/jit(_where)/select_n | solution.py:49
  33.1 0.0 copy-done
  33.1 0.0 copy-start.3
  33.1 8.1 %fusion.37 = f32[1,3,6,64,384]{4,0,3,2,1:T(1,128)S(1)} fusion(bf16[1,5,8,64,16]{4,0,3,2,1:T(2,128)(2,1)S(1)} %copy.28, bf16[3,3,3,16,384]{4,3,2,1,0:T(8,128)(2,1)S(1)} %copy-done), kind=kOutput, calls=%fused_computation.93 | convolution fusion | flops 378224640 | bytes 2183168 | tf_op jit(solution)/shard_map/conv_general_dilated | solution.py:53
  41.1 0.0 copy-done.3
  41.1 0.0 copy-start.4
  41.2 0.2 multiply_reduce_fusion
  41.4 0.0 copy-start.1
  41.4 0.4 copy-done.4
  41.8 1.5 %multiply_convert_fusion.fresh = bf16[3,6,64,384]{3,2,1,0:T(8,128)(2,1)} fusion(f32[1,3,6,64,384]{4,0,3,2,1:T(1,128)S(1)} %fusion.37, f32[384]{0:T(512)S(1)} %copy-done.4, f32[3,6,64]{2,1,0:T(8,128)S(1)} %add_rsqrt_fusion, f32[384]{0:T(512)S(1)} %copy-done.3), kind=kLoop, calls=%fused_computation.9 | loop fusion | flops 3538944 | bytes 2661888 | tf_op jit(solution)/shard_map/convert_element_type | solution.py:66
  43.3 0.0 collective-permute-done
  43.3 0.0 collective-permute-done.1
  43.3 0.0 copy-done.1
  43.3 0.9 %pad_maximum_fusion.cached = bf16[2,6,64,384]{3,2,1,0:T(8,128)(2,1)} fusion(bf16[2,1,64,384]{3,2,1,0:T(8,128)(2,1)S(1)} %collective-permute-done.1, bf16[2,4,64,384]{3,2,1,0:T(8,128)(2,1)S(1)} %copy-done.1, bf16[2,1,64,384]{3,2,1,0:T(8,128)(2,1)S(1)} %collective-permute-done), kind=kLoop, calls=%fused_computation.18 | loop fusion | flops 589824 | bytes 1179648 | tf_op jit(solution)/shard_map/concatenate | solution.py:24
  44.3 16.3 %shard_map.130 = (bf16[3,8,192,128]{3,2,1,0:T(8,128)(2,1)}, bf16[2,4,64,384]{3,2,1,0:T(8,128)(2,1)}) custom-call(s32[3]{0:T(128)} %pad_add_fusion.info, bf16[2,6,64,384]{3,2,1,0:T(8,128)(2,1)} %pad_maximum_fusion.cached, bf16[3,6,64,384]{3,2,1,0:T(8,128)(2,1)} %multiply_convert_fusion.fresh, bf16[3,3,3,192,384]{4,3,2,1,0:T(8,128)(2,1)} %bitcast.41, ...), custom_call_target="tpu_custom_call" | custom-call | flops 5435817984 | bytes 8000000 | tf_op jit(solution)/shard_map/pallas_call | solution.py:158
  (11 shorter events, 0.2 us)
Async XLA Ops:
  0.6 32.4 %copy-start = (bf16[3,3,3,16,384]{4,3,2,1,0:T(8,128)(2,1)S(1)}, bf16[3,3,3,16,384]{4,3,2,1,0:T(8,128)(2,1)}, u32[]{:S(2)}) copy-start(bf16[3,3,3,16,384]{4,3,2,1,0:T(8,128)(2,1)} %param.17) | copy-start | bytes 995332
  0.6 18.4 %copy-start.6 = (s32[8]{0:T(128)S(1)}, s32[8]{0:T(128)}, u32[]{:S(2)}) copy-start(s32[8]{0:T(128)} %param.13) | copy-start | bytes 100
  5.3 16.5 %copy-start.7 = (s32[8]{0:T(128)S(1)}, s32[8]{0:T(128)}, u32[]{:S(2)}) copy-start(s32[8]{0:T(128)} %param.14) | copy-start | bytes 100
  5.3 18.2 %copy-start.2 = (bf16[2,4,1024]{2,1,0:T(4,128)(2,1)S(1)}, bf16[2,4,1024]{2,1,0:T(4,128)(2,1)}, u32[]{:S(2)}) copy-start(bf16[2,4,1024]{2,1,0:T(4,128)(2,1)} %param.15) | copy-start | bytes 49156
  6.1 18.5 %all-to-all-start = ((bf16[16,2,384]{2,1,0:T(2,128)(2,1)}), bf16[16,2,384]{2,1,0:T(2,128)(2,1)S(1)}, u32[]{:S(2)}, u32[]{:S(2)}) async-start(bf16[16,2,384]{2,1,0:T(2,128)(2,1)} %reshape.192), calls=%async_computation | async-start | bytes 49152 | tf_op jit(solution)/shard_map/all_to_all | solution.py:219
  13.5 10.3 %copy-start.5 = (f32[192]{0:T(256)S(1)}, f32[192]{0:T(256)}, u32[]{:S(2)}) copy-start(f32[192]{0:T(256)} %param.21) | copy-start | bytes 2308
  14.5 28.9 %collective-permute-start = (bf16[2,1,64,384]{3,2,1,0:T(8,128)(2,1)S(1)}, bf16[2,1,64,384]{3,2,1,0:T(8,128)(2,1)S(1)}, u32[]{:S(2)}, u32[]{:S(2)}) collective-permute-start(bf16[2,1,64,384]{3,2,1,0:T(8,128)(2,1)S(1)} %get-tuple-element.31), channel_id=1, source_target_pairs={{0,1},{1,2},{2,3},{3,4},{4,5},{5,6},{6,7},{7,8},{8,9},{9,10},{10,1... | collective-permute-start | bytes 294920 | tf_op jit(solution)/shard_map/ppermute | solution.py:22
  14.9 28.4 %collective-permute-start.1 = (bf16[2,1,64,384]{3,2,1,0:T(8,128)(2,1)S(1)}, bf16[2,1,64,384]{3,2,1,0:T(8,128)(2,1)S(1)}, u32[]{:S(2)}, u32[]{:S(2)}) collective-permute-start(bf16[2,1,64,384]{3,2,1,0:T(8,128)(2,1)S(1)} %get-tuple-element.32), channel_id=1, source_target_pairs={{1,0},{2,1},{3,2},{4,3},{5,4},{6,5},{7,6},{8,7},{9,8},{10,9},{11,1... | collective-permute-start | bytes 294920 | tf_op jit(solution)/shard_map/ppermute | solution.py:23
  25.5 2.1 %collective-permute-start.3 = (bf16[5,2,64,16]{2,3,1,0:T(8,128)(2,1)S(1)}, bf16[5,2,64,16]{2,3,1,0:T(8,128)(2,1)S(1)}, u32[]{:S(2)}, u32[]{:S(2)}) collective-permute-start(bf16[5,2,64,16]{2,3,1,0:T(8,128)(2,1)S(1)} %get-tuple-element.34), channel_id=1, source_target_pairs={{1,0},{2,1},{3,2},{4,3},{5,4},{6,5},{7,6},{8,7},{9,8},{10,9},{11,1... | collective-permute-start | bytes 61448 | tf_op jit(solution)/shard_map/ppermute | solution.py:23
  26.0 6.1 %collective-permute-start.2 = (bf16[5,2,64,16]{2,3,1,0:T(8,128)(2,1)S(1)}, bf16[5,2,64,16]{2,3,1,0:T(8,128)(2,1)S(1)}, u32[]{:S(2)}, u32[]{:S(2)}) collective-permute-start(bf16[5,2,64,16]{2,3,1,0:T(8,128)(2,1)S(1)} %get-tuple-element.33), channel_id=1, source_target_pairs={{0,1},{1,2},{2,3},{3,4},{4,5},{5,6},{6,7},{7,8},{8,9},{9,10},{10,1... | collective-permute-start | bytes 61448 | tf_op jit(solution)/shard_map/ppermute | solution.py:22
  33.1 8.1 %copy-start.3 = (f32[384]{0:T(512)S(1)}, f32[384]{0:T(512)}, u32[]{:S(2)}) copy-start(f32[384]{0:T(512)} %param.18) | copy-start | bytes 4612
  41.1 0.7 %copy-start.4 = (f32[384]{0:T(512)S(1)}, f32[384]{0:T(512)}, u32[]{:S(2)}) copy-start(f32[384]{0:T(512)} %param.19) | copy-start | bytes 4612
  41.4 1.9 %copy-start.1 = (bf16[2,4,64,384]{3,2,1,0:T(8,128)(2,1)S(1)}, bf16[2,4,64,384]{3,2,1,0:T(8,128)(2,1)}, u32[]{:S(2)}) copy-start(bf16[2,4,64,384]{3,2,1,0:T(8,128)(2,1)} %param.16) | copy-start | bytes 1179652
